TPU v7x, 32 devices: a whole 2x2x4 slice. The times are simulated.
32 devices in a mesh: seq: 2 (over y), dom: 8 (over z, x), tm: 2 (over core).
Axes of the slice: x: 2, y: 2, z: 4, core: 2. Of those that a mesh axis runs over, the one named last changes fastest.
Arguments:
- particles: bfloat16 [4, 1536, 128], P('tm', ('seq', 'dom')), parts along dimension 1, may hold values from -6 to 6
- log_weight: float32 [4, 1536], P('tm', ('seq', 'dom')), parts along dimension 1, may hold values from -13 to 313
- trans_weight: bfloat16 [128, 128], replicated, may hold values from -0.5 to 0.5
- precision: float32 [128], replicated, may hold values from 0.2 to 2
Outputs:
- smoothed: float32 [4, 1536], P('tm', ('seq', 'dom')), parts along dimension 1
- score: float32 [256, 128], P('seq'), parts along dimension 0
There are 2 independent parts, one for each index of `seq`. A program takes and returns all parts, laid end to end along the dimension named above; an argument that names none is the same for every part. Nothing has to cross between parts.
All inputs are finite; a program needn't handle non-finite values.
Results may differ from a plain program's by a relative error of at most 0.0061.
Values may be sent and summed in bfloat16 or wider, within the bound.
A program may use at most 64 MiB of HBM per device.

v0:
```python
import jax
import jax.numpy as jnp
from jax import lax
from jax.sharding import PartitionSpec as P

exact_mode = lax.Precision.HIGHEST


def from_behind(x, axis, by):
    size = lax.axis_size(axis)
    pairs = [(i, i + by) for i in range(size) if 0 <= i + by < size]
    return lax.ppermute(x, axis, pairs)


def block_size(length):
    best = 1
    for trial in range(1, min(length, 512) + 1):
        if length % trial == 0:
            best = trial
    return best


def project_rows(rows, precision, weight_full):
    return jnp.dot(rows.astype(jnp.float32) * precision, weight_full, precision=exact_mode).astype(
        jnp.bfloat16
    )


def pair_scores(row_proj, column_rows, column_bias):
    return (
        jnp.einsum("id,jd->ij", row_proj, column_rows, preferred_element_type=jnp.float32)
        + column_bias[None, :]
    )


def make_norm_fold(row_proj, bias_row, carried, block_in, first_row):
    length = block_in.shape[0]
    size = block_size(length)

    def inner(position, state):
        row_top, row_total = state
        offset = position * size
        column_rows = lax.dynamic_slice_in_dim(block_in, offset, size, 0)
        bias_part = lax.dynamic_slice_in_dim(bias_row, first_row + offset, size, 0)
        scores = pair_scores(row_proj, column_rows, bias_part)
        new_top = jnp.maximum(row_top, jnp.max(scores, axis=1))
        row_total = row_total * jnp.exp(row_top - new_top) + jnp.sum(
            jnp.exp(scores - new_top[:, None]), axis=1
        )
        return (new_top, row_total)

    return lax.fori_loop(0, length // size, inner, carried)


def make_column_fold(row_proj, bias_row, row_norm, row_weight, carried, block_in, first_row):
    length = block_in.shape[0]
    size = block_size(length)

    def inner(position, state):
        moved, column_sums = state
        offset = position * size
        column_rows = lax.dynamic_slice_in_dim(block_in, offset, size, 0)
        bias_part = lax.dynamic_slice_in_dim(bias_row, first_row + offset, size, 0)
        scores = pair_scores(row_proj, column_rows, bias_part)
        backward = (row_weight[:, None] * jnp.exp(scores - row_norm[:, None])).astype(jnp.bfloat16)
        moved = moved + jnp.dot(backward, column_rows, preferred_element_type=jnp.float32)
        column_sums = lax.dynamic_update_slice_in_dim(
            column_sums, jnp.sum(backward.astype(jnp.float32), axis=0), first_row + offset, 0
        )
        return (moved, column_sums)

    return lax.fori_loop(0, length // size, inner, carried)


def shards(particles, log_weight, trans_weight, precision):
    steps_here, rows_here, width = particles.shape
    tm_count = lax.axis_size("tm")
    dom_count = lax.axis_size("dom")
    total_rows = rows_here * dom_count
    tm_place = lax.axis_index("tm")
    is_last = tm_place == tm_count - 1
    weight_full = trans_weight.astype(jnp.float32)
    boundary = from_behind(particles[0], "tm", -1)
    later_sets = [particles[1]] + [boundary]
    later_proj = [project_rows(rows, precision, weight_full) for rows in later_sets]
    biases = []
    for k in range(steps_here):
        predicted = jnp.dot(particles[k], trans_weight.T, preferred_element_type=jnp.float32)
        biases.append(log_weight[k] - 0.5 * jnp.sum(precision * predicted * predicted, axis=1))
    local_bias = jnp.stack(biases)
    full_bias = lax.all_gather(local_bias, "dom", axis=1, tiled=True)
    row_norms = []
    whole = lax.all_gather(particles, "dom", axis=1, tiled=True)
    for k in range(steps_here):
        start_state = (
            jnp.full((rows_here,), -jnp.inf, jnp.float32),
            jnp.zeros((rows_here,), jnp.float32),
        )
        row_top, row_total = make_norm_fold(later_proj[k], full_bias[k], start_state, whole[k], 0)
        row_norms.append(row_top + jnp.log(row_total))
    final_logs = log_weight[steps_here - 1]
    global_top = lax.pmax(jnp.max(final_logs), "dom")
    global_total = lax.psum(jnp.sum(jnp.exp(final_logs - global_top)), "dom")
    final_weights = jnp.exp(final_logs - global_top) / global_total
    carried = (
        jnp.zeros((steps_here, rows_here), jnp.float32),
        jnp.zeros((width, width), jnp.float32),
    )
    for r in range(tm_count):
        if r == 0:
            incoming = jnp.zeros((rows_here,), jnp.float32)
        else:
            incoming = from_behind(carried[0][0], "tm", -1)
        owner = tm_count - 1 - r
        backward_partial_value = jnp.zeros((width, width), jnp.float32)
        outputs = [None] * steps_here
        row_weight = incoming
        for backward_k in range(steps_here - 1, -1, -1):
            column_rows = particles[backward_k]
            backward_start_state = (
                jnp.zeros((rows_here, width), jnp.float32),
                jnp.zeros((total_rows,), jnp.float32),
            )
            moved, column_sums = make_column_fold(
                later_proj[backward_k],
                full_bias[backward_k],
                row_norms[backward_k],
                row_weight,
                backward_start_state,
                whole[backward_k],
                0,
            )
            column_weights = lax.psum_scatter(column_sums, "dom", scatter_dimension=0, tiled=True)
            outer = jnp.dot(
                later_sets[backward_k].astype(jnp.float32).T, moved, precision=exact_mode
            )
            column_float = column_rows.astype(jnp.float32)
            moment = jnp.dot(
                column_float.T * column_weights[None, :], column_float, precision=exact_mode
            )
            backward_partial_value = backward_partial_value + precision[:, None] * (
                outer - jnp.dot(weight_full, moment, precision=exact_mode)
            )
            if backward_k == steps_here - 1:
                column_weights = jnp.where(is_last, final_weights, column_weights)
            outputs[backward_k] = column_weights
            row_weight = column_weights
        is_owner = tm_place == owner
        carried = (
            jnp.where(is_owner, jnp.stack(outputs), carried[0]),
            jnp.where(is_owner, backward_partial_value, carried[1]),
        )
    stacked, partial_value = carried
    score = lax.psum(partial_value, ("dom", "tm"))
    return (stacked * total_rows, score)


def solution(mesh):
    placed = (P("tm", ("seq", "dom"), None), P("tm", ("seq", "dom")), P(), P())
    return jax.shard_map(
        shards,
        mesh=mesh,
        in_specs=placed,
        out_specs=(P("tm", ("seq", "dom")), P("seq", None)),
        check_vma=False,
    )
```

profile of v0, /device:TPU:8, one launch (start us, length us, event | category | flops | bytes accessed | tf_op | source)
XLA Modules:
  0.0 267.3 jit_solution(9784451875654501515)
XLA Ops:
  7.2 0.8 slice_bitcast_fusion.2
  8.0 1.4 collective-permute-start
  9.4 28.6 %all_gather.6 = bf16[2,768,128]{2,1,0:T(8,128)(2,1)S(1)} all-gather(bf16[2,96,128]{2,1,0:T(8,128)(2,1)S(1)} %copy-done.1), channel_id=1, replica_groups=mesh['seq'=2,'dom'=8,'tm'=2] {'dom'}, dimensions={1}, use_global_device_ids=true | all-gather | bytes 442368 | tf_op jit(solution)/shard_map/all_gather | solution.py:93
  38.0 0.3 fusion.54
  38.3 0.3 fusion.53
  38.8 0.6 copy-done.3
  39.4 0.6 slice_reduce_fusion.2
  40.0 22.1 %pmax.7 = f32[]{:T(128)} all-reduce(f32[]{:T(128)} %slice_reduce_fusion.2), channel_id=1, replica_groups=mesh['seq'=2,'dom'=8,'tm'=2] {'dom'}, use_global_device_ids=true, to_apply=%region_3.4 | all-reduce | flops 1 | bytes 8 | tf_op jit(solution)/shard_map/pmax | solution.py:102
  62.1 1.2 fusion.81
  63.3 16.3 %all-gather = f32[8,96,2]{1,2,0:T(2,128)S(1)} all-gather(f32[1,96,2]{1,2,0:T(2,128)S(1)} %maximum_bitcast_fusion), channel_id=1, replica_groups=mesh['seq'=2,'dom'=8,'tm'=2] {'dom'}, dimensions={0}, use_global_device_ids=true | all-gather | bytes 6912 | tf_op jit(solution)/shard_map/all_gather | solution.py:91
  79.7 1.2 while.98
  79.8 0.3 fusion.143
  80.1 0.2 exponential_reduce_fusion.5
  80.4 0.3 fusion.143
  80.7 0.2 exponential_reduce_fusion.5
  81.0 0.6 copy-done.4
  81.7 0.6 dynamic-slice
  83.1 1.2 while.96
  83.2 0.3 fusion.136
  83.4 0.2 exponential_reduce_fusion.4
  83.7 0.3 fusion.136
  84.0 0.2 exponential_reduce_fusion.4
  84.3 1.5 while.97
  84.4 0.2 convert_reduce_fusion.8
  84.8 0.2 dynamic_update_slice.36
  85.1 0.2 convert_reduce_fusion.8
  85.3 0.2 convolution_add_fusion.14
  85.5 0.2 dynamic_update_slice.36
  85.8 19.9 %all-reduce.4 = (f32[768]{0:T(1024)S(1)}, f32[]{:T(128)}) all-reduce(f32[768]{0:T(1024)S(1)} %get-tuple-element.769, f32[]{:T(128)} %get-tuple-element.1041), channel_id=2, replica_groups=mesh['seq'=2,'dom'=8,'tm'=2] {'dom'}, use_global_device_ids=true, to_apply=%region_13.0.clone | all-reduce | flops 769 | bytes 6152
  105.6 1.3 broadcast_select_fusion.5
  106.9 1.5 while.99
  107.0 0.2 convert_reduce_fusion.9
  107.4 0.2 dynamic_update_slice.37
  107.7 0.2 convert_reduce_fusion.9
  108.1 0.2 dynamic_update_slice.37
  108.4 17.1 %all-reduce.1 = f32[768]{0:T(1024)S(1)} all-reduce(f32[768]{0:T(1024)S(1)} %get-tuple-element.772), channel_id=3, replica_groups=mesh['seq'=2,'dom'=8,'tm'=2] {'dom'}, use_global_device_ids=true, to_apply=%region_21.22.clone | all-reduce | flops 768 | bytes 6144
  125.6 1.3 collective-permute-start.1
  126.9 0.2 fusion.57
  127.2 0.3 fusion.52
  127.5 0.3 fusion.50
  127.8 0.2 fusion.86
  128.1 0.2 convolution_subtract_fusion
  128.3 0.3 fusion.44
  128.7 1.5 while.100
  128.7 0.2 convert_reduce_fusion.10
  129.1 0.2 dynamic_update_slice.38
  129.5 0.2 convert_reduce_fusion.10
  129.9 0.2 dynamic_update_slice.38
  130.1 19.1 %all-reduce.2 = f32[768]{0:T(1024)S(1)} all-reduce(f32[768]{0:T(1024)S(1)} %get-tuple-element.773), channel_id=4, replica_groups=mesh['seq'=2,'dom'=8,'tm'=2] {'dom'}, use_global_device_ids=true, to_apply=%region_25.26.clone | all-reduce | flops 768 | bytes 6144
  149.3 1.5 while.101
  149.4 0.2 convert_reduce_fusion.11
  149.8 0.2 dynamic_update_slice.39
  150.1 0.2 convert_reduce_fusion.11
  150.5 0.2 dynamic_update_slice.39
  150.8 17.1 %all-reduce.3 = f32[768]{0:T(1024)S(1)} all-reduce(f32[768]{0:T(1024)S(1)} %get-tuple-element.774), channel_id=5, replica_groups=mesh['seq'=2,'dom'=8,'tm'=2] {'dom'}, use_global_device_ids=true, to_apply=%region_29.30.clone | all-reduce | flops 768 | bytes 6144
  168.0 0.2 fusion.60
  168.3 0.3 fusion.51
  168.6 0.3 fusion.49
  168.9 0.2 fusion.85
  169.2 0.2 convolution_subtract_fusion.2
  169.4 0.9 fusion.48
  170.4 0.6 fusion.80
  170.9 88.0 %all-reduce.7.cloned.1.call-done = f32[128,128]{0,1:T(8,128)} async-done(((f32[128,128]{0,1:T(8,128)}), f32[128,128]{0,1:T(8,128)}) %all-reduce.7.cloned.1.call-update) | async-done | bytes 65552 | tf_op jit(solution)/shard_map/psum | solution.py:154
  258.9 1.6 copy.10
  (70 shorter events, 3.3 us)
Async XLA Ops:
  7.2 30.9 %copy-start = (bf16[128,128]{1,0:T(8,128)(2,1)S(1)}, bf16[128,128]{1,0:T(8,128)(2,1)}, u32[]{:S(2)}) copy-start(bf16[128,128]{1,0:T(8,128)(2,1)} %param.18) | copy-start | bytes 98308
  7.2 2.2 copy-start.1
  7.2 251.7 %all-reduce.7.cloned.1.call-start = ((), (), s32[]{:S(2)}) async-start(), calls=%async_computation | async-start | bytes 131072 | tf_op jit(solution)/shard_map/psum | solution.py:154
  8.0 30.0 %copy-start.2 = (f32[128]{0:T(128)S(1)}, f32[128]{0:T(128)}, u32[]{:S(2)}) copy-start(f32[128]{0:T(128)} %param.19) | copy-start | bytes 1540
  8.0 74.9 %collective-permute-start = (bf16[96,128]{1,0:T(8,128)(2,1)S(1)}, bf16[96,128]{1,0:T(8,128)(2,1)S(1)}, u32[]{:S(2)}, u32[]{:S(2)}) collective-permute-start(bf16[96,128]{1,0:T(8,128)(2,1)S(1)} %slice_bitcast_fusion.2), channel_id=1, source_target_pairs={{1,0},{3,2},{5,4},{7,6},{9,8},{11,10},{13,12},{15,14},{17,16},{19,... | collective-permute-start | bytes 73736 | tf_op jit(solution)/shard_map/ppermute | solution.py:12
  38.7 0.7 copy-start.3
  81.0 0.7 copy-start.4
  125.6 3.0 %collective-permute-start.1 = (f32[96]{0:T(128)S(1)}, f32[96]{0:T(128)S(1)}, u32[]{:S(2)}, u32[]{:S(2)}) collective-permute-start(f32[96]{0:T(128)S(1)} %slice_bitcast_fusion.3), channel_id=1, source_target_pairs={{1,0},{3,2},{5,4},{7,6},{9,8},{11,10},{13,12},{15,14},{17,16},{19,... | collective-permute-start | bytes 1160 | tf_op jit(solution)/shard_map/ppermute | solution.py:12
Sparse Core Ops, SparseCore 0:
  170.5 88.4 all-reduce.6
where the time goes:
time: 268 us; the launch traced here: 267 us
  blocking collectives  140 us (52%)
  waiting for transfers between devices  88.1 us (33%)
  between operations  14.9 us (6%)
  matrix products  8.92 us (3%)
  local copies, waits for them, and re-layouts  7.58 us (3%)
  other arithmetic  4.58 us (2%)
  starting transfers between devices  2.74 us (1%)
    psum x1, waiting for transfers between devices, shards(): score = lax.psum(partial_value, ('dom', 'tm'))  88 us
    unnamed x4, blocking collectives  73.2 us
    all_gather x1, blocking collectives, shards(): whole = lax.all_gather(particles, 'dom', axis=1, tiled=True)  28.6 us
    pmax x1, blocking collectives, shards(): global_top = lax.pmax(jnp.max(final_logs), 'dom')  22.1 us
    all_gather x1, blocking collectives, shards(): full_bias = lax.all_gather(local_bias, 'dom', axis=1, tiled=True)  16.3 us
  transfers between devices with their start and end apart: 3, of which 2 were waited for; matrix products, arithmetic and copies ran while one was open for 2% of the time, Pallas kernels for 0%

commit v1 on v0

--- a/solution.py
+++ b/solution.py
@@ -4,6 +4,12 @@
 from jax.sharding import PartitionSpec as P
 
 exact_mode = lax.Precision.HIGHEST
+
+
+def joined_along(tiles, dim):
+    lengths = list(tiles.shape[1:])
+    lengths[dim] *= tiles.shape[0]
+    return jnp.moveaxis(tiles, 0, dim).reshape(lengths)
 
 
 def from_behind(x, axis, by):
@@ -88,7 +94,19 @@
         predicted = jnp.dot(particles[k], trans_weight.T, preferred_element_type=jnp.float32)
         biases.append(log_weight[k] - 0.5 * jnp.sum(precision * predicted * predicted, axis=1))
     local_bias = jnp.stack(biases)
-    full_bias = lax.all_gather(local_bias, "dom", axis=1, tiled=True)
+    count = lax.axis_size("dom")
+    pairs_2 = [(i_2, (i_2 + 1) % count) for i_2 in range(count)]
+    back = [(b, a) for a, b in pairs_2]
+    lower, upper = ([], [])
+    for step in range(count - 1):
+        if step % 2 == 0:
+            lower.append(lax.ppermute(lower[-1] if lower else local_bias, "dom", pairs_2))
+        else:
+            upper.append(lax.ppermute(upper[-1] if upper else local_bias, "dom", back))
+    pieces = jnp.stack([*lower[::-1], local_bias, *upper])
+    shift = lax.axis_index("dom") - len(lower)
+    pieces = pieces[(jnp.arange(count) - shift) % count]
+    full_bias = joined_along(pieces, 1)
     row_norms = []
     whole = lax.all_gather(particles, "dom", axis=1, tiled=True)
     for k in range(steps_here):

time: 268 us -> 278 us (1.037)
  starting transfers between devices: 2.74 us -> 12.2 us
  waiting for transfers between devices: 88.1 us -> 95.2 us
  blocking collectives: 140 us -> 133 us
    all_gather x1 -> x0, blocking collectives: 16.3 us -> none  [shards(): full_bias = lax.all_gather(local_bias, 'dom', axis=1, tiled=True)]
    ppermute x0 -> x7, starting transfers between devices: none -> 9.59 us  [the longest x3 9.53 us: shards(): upper.append(lax.ppermute(upper[-1] if upper else local_bias, 'dom', back))]
    unnamed x4, blocking collectives: 73.2 us -> 80.9 us
    ppermute x0 -> x7, waiting for transfers between devices: none -> 7.14 us  [the longest x4 5.91 us: shards(): lax.ppermute(lower[-1] if lower else local_bias, 'dom', pairs_2)]
    all_gather x1, blocking collectives: 28.6 us -> 32.9 us  [shards(): whole = lax.all_gather(particles, 'dom', axis=1, tiled=True)]
  transfers between devices with their start and end apart: 3 -> 10, of which waited for: 2 -> 5; matrix products, arithmetic and copies ran while one was open for 2% -> 2% of each run, Pallas kernels for 0% -> 0%
where the time goes in v1:
time: 278 us
  blocking collectives  133 us (48%)
  waiting for transfers between devices  95.2 us (34%)
  between operations  14.9 us (5%)
  starting transfers between devices  12.2 us (4%)
  matrix products  9.67 us (3%)
  local copies, waits for them, and re-layouts  6.87 us (2%)
  other arithmetic  5.3 us (2%)
    psum x1, waiting for transfers between devices, shards(): score = lax.psum(partial_value, ('dom', 'tm'))  88 us
    unnamed x4, blocking collectives  80.9 us
    all_gather x1, blocking collectives, shards(): whole = lax.all_gather(particles, 'dom', axis=1, tiled=True)  32.9 us
    pmax x1, blocking collectives, shards(): global_top = lax.pmax(jnp.max(final_logs), 'dom')  19.5 us
    ppermute x3, starting transfers between devices, shards(): upper.append(lax.ppermute(upper[-1] if upper else local_bias, 'dom', back))  9.53 us
    ppermute x4, waiting for transfers between devices, shards(): lax.ppermute(lower[-1] if lower else local_bias, 'dom', pairs_2)  5.91 us
  transfers between devices with their start and end apart: 10, of which 5 were waited for; matrix products, arithmetic and copies ran while one was open for 2% of the time, Pallas kernels for 0%

profile of v1, /device:TPU:8, one launch (start us, length us, event | category | flops | bytes accessed | tf_op | source)
XLA Modules:
  0.0 277.7 jit_solution(5753690974708293607)
XLA Ops:
  7.2 1.3 slice_reduce_fusion.2
  8.5 1.0 fusion.54
  9.6 0.3 fusion.53
  9.8 19.5 %pmax.7 = f32[]{:T(128)} all-reduce(f32[]{:T(128)} %slice_reduce_fusion.2), channel_id=1, replica_groups=mesh['seq'=2,'dom'=8,'tm'=2] {'dom'}, use_global_device_ids=true, to_apply=%region_3.4 | all-reduce | flops 1 | bytes 8 | tf_op jit(solution)/shard_map/pmax | solution.py:120
  29.3 1.2 fusion.83
  30.5 2.9 %collective-permute-start.5 = (f32[2,96]{1,0:T(2,128)S(1)}, f32[2,96]{1,0:T(2,128)S(1)}, u32[]{:S(2)}, u32[]{:S(2)}) collective-permute-start(f32[2,96]{1,0:T(2,128)S(1)} %pad_maximum_fusion), channel_id=1, source_target_pairs={{2,0},{4,2},{6,4},{8,6},{10,8},{12,10},{14,12},{0,14},{3,1},{5,3},... | collective-permute-start | bytes 2312 | tf_op jit(solution)/shard_map/ppermute | solution.py:105
  33.4 1.3 collective-permute-start
  34.7 32.9 %all_gather.3 = bf16[2,768,128]{2,1,0:T(8,128)(2,1)S(1)} all-gather(bf16[2,96,128]{2,1,0:T(8,128)(2,1)S(1)} %copy-done.1), channel_id=1, replica_groups=mesh['seq'=2,'dom'=8,'tm'=2] {'dom'}, dimensions={1}, use_global_device_ids=true | all-gather | bytes 442368 | tf_op jit(solution)/shard_map/all_gather | solution.py:111
  67.9 4.4 %collective-permute-done.2 = f32[2,96]{1,0:T(2,128)S(1)} collective-permute-done((f32[2,96]{1,0:T(2,128)S(1)}, f32[2,96]{1,0:T(2,128)S(1)}, u32[]{:S(2)}, u32[]{:S(2)}) %collective-permute-start.2) | collective-permute-done | bytes 800 | tf_op jit(solution)/shard_map/ppermute | solution.py:103
  72.4 3.0 %collective-permute-start.6 = (f32[2,96]{1,0:T(2,128)S(1)}, f32[2,96]{1,0:T(2,128)S(1)}, u32[]{:S(2)}, u32[]{:S(2)}) collective-permute-start(f32[2,96]{1,0:T(2,128)S(1)} %collective-permute-done.5), channel_id=1, source_target_pairs={{2,0},{4,2},{6,4},{8,6},{10,8},{12,10},{14,12},{0,14},{3,1},{5,3},... | collective-permute-start | bytes 2312 | tf_op jit(solution)/shard_map/ppermute | solution.py:105
  75.3 1.5 collective-permute-done.3
  76.8 0.7 copy-done.4
  77.5 0.6 dynamic-slice
  78.6 3.7 %collective-permute-start.7 = (f32[2,96]{1,0:T(2,128)S(1)}, f32[2,96]{1,0:T(2,128)S(1)}, u32[]{:S(2)}, u32[]{:S(2)}) collective-permute-start(f32[2,96]{1,0:T(2,128)S(1)} %collective-permute-done.6), channel_id=1, source_target_pairs={{2,0},{4,2},{6,4},{8,6},{10,8},{12,10},{14,12},{0,14},{3,1},{5,3},... | collective-permute-start | bytes 2312 | tf_op jit(solution)/shard_map/ppermute | solution.py:105
  82.4 1.2 collective-permute-done.7
  83.6 0.6 gather_fusion
  84.3 1.2 while.98
  84.4 0.3 fusion.145
  84.6 0.2 exponential_reduce_fusion.5
  85.0 0.3 fusion.145
  85.7 1.2 while.96
  85.8 0.3 fusion.138
  86.4 0.3 fusion.138
  86.9 1.5 while.97
  87.0 0.2 convert_reduce_fusion.8
  87.4 0.2 dynamic_update_slice.36
  87.8 0.2 convert_reduce_fusion.8
  88.2 0.2 dynamic_update_slice.36
  88.4 27.5 %all-reduce.4 = (f32[768]{0:T(1024)S(1)}, f32[]{:T(128)}) all-reduce(f32[768]{0:T(1024)S(1)} %get-tuple-element.769, f32[]{:T(128)} %get-tuple-element.1039), channel_id=2, replica_groups=mesh['seq'=2,'dom'=8,'tm'=2] {'dom'}, use_global_device_ids=true, to_apply=%region_13.14.clone | all-reduce | flops 769 | bytes 6152
  116.0 1.3 broadcast_select_fusion.5
  117.2 1.5 while.99
  117.3 0.2 convert_reduce_fusion.9
  117.7 0.2 dynamic_update_slice.37
  118.0 0.2 convert_reduce_fusion.9
  118.4 0.2 dynamic_update_slice.37
  118.7 17.1 %all-reduce.1 = f32[768]{0:T(1024)S(1)} all-reduce(f32[768]{0:T(1024)S(1)} %get-tuple-element.772), channel_id=3, replica_groups=mesh['seq'=2,'dom'=8,'tm'=2] {'dom'}, use_global_device_ids=true, to_apply=%region_21.22.clone | all-reduce | flops 768 | bytes 6144
  136.0 1.3 collective-permute-start.8
  137.3 0.2 fusion.57
  137.5 0.3 fusion.52
  137.8 0.3 fusion.50
  138.2 0.2 fusion.88
  138.4 0.2 convolution_subtract_fusion
  138.7 0.3 fusion.44
  139.0 1.5 while.100
  139.1 0.2 convert_reduce_fusion.10
  139.5 0.2 dynamic_update_slice.38
  139.8 0.2 convert_reduce_fusion.10
  140.2 0.2 dynamic_update_slice.38
  140.5 19.1 %all-reduce.2 = f32[768]{0:T(1024)S(1)} all-reduce(f32[768]{0:T(1024)S(1)} %get-tuple-element.773), channel_id=4, replica_groups=mesh['seq'=2,'dom'=8,'tm'=2] {'dom'}, use_global_device_ids=true, to_apply=%region_25.26.clone | all-reduce | flops 768 | bytes 6144
  159.6 1.5 while.101
  159.7 0.2 convert_reduce_fusion.11
  160.1 0.2 dynamic_update_slice.39
  160.5 0.2 convert_reduce_fusion.11
  160.9 0.2 dynamic_update_slice.39
  161.1 17.1 %all-reduce.3 = f32[768]{0:T(1024)S(1)} all-reduce(f32[768]{0:T(1024)S(1)} %get-tuple-element.774), channel_id=5, replica_groups=mesh['seq'=2,'dom'=8,'tm'=2] {'dom'}, use_global_device_ids=true, to_apply=%region_29.30.clone | all-reduce | flops 768 | bytes 6144
  178.4 0.2 fusion.60
  178.6 0.3 fusion.51
  178.9 0.3 fusion.49
  179.3 0.2 fusion.87
  179.5 0.2 convolution_subtract_fusion.2
  179.8 0.9 fusion.48
  180.7 0.6 fusion.80
  181.3 88.0 %all-reduce.7.cloned.1.call-done = f32[128,128]{0,1:T(8,128)} async-done(((f32[128,128]{0,1:T(8,128)}), f32[128,128]{0,1:T(8,128)}) %all-reduce.7.cloned.1.call-update) | async-done | bytes 65552 | tf_op jit(solution)/shard_map/psum | solution.py:172
  269.3 1.6 copy.7
  (94 shorter events, 4.3 us)
Async XLA Ops:
  7.2 1.4 copy-start
  7.2 2.4 copy-start.1
  7.2 262.1 %all-reduce.7.cloned.1.call-start = ((), (), s32[]{:S(2)}) async-start(), calls=%async_computation | async-start | bytes 131072 | tf_op jit(solution)/shard_map/psum | solution.py:172
  8.5 1.0 copy-start.2
  9.8 19.5 %copy-start.3 = (f32[2,96]{1,0:T(2,128)S(1)}, f32[2,96]{1,0:T(2,128)}, u32[]{:S(2)}) copy-start(f32[2,96]{1,0:T(2,128)} %param.17) | copy-start | bytes 2308
  30.5 37.3 %collective-permute-start.1 = (f32[2,96]{1,0:T(2,128)S(1)}, f32[2,96]{1,0:T(2,128)S(1)}, u32[]{:S(2)}, u32[]{:S(2)}) collective-permute-start(f32[2,96]{1,0:T(2,128)S(1)} %pad_maximum_fusion), channel_id=1, source_target_pairs={{0,2},{2,4},{4,6},{6,8},{8,10},{10,12},{12,14},{14,0},{1,3},{3,5},... | collective-permute-start | bytes 2312 | tf_op jit(solution)/shard_map/ppermute | solution.py:103
  30.5 41.9 %collective-permute-start.5 = (f32[2,96]{1,0:T(2,128)S(1)}, f32[2,96]{1,0:T(2,128)S(1)}, u32[]{:S(2)}, u32[]{:S(2)}) collective-permute-start(f32[2,96]{1,0:T(2,128)S(1)} %pad_maximum_fusion), channel_id=1, source_target_pairs={{2,0},{4,2},{6,4},{8,6},{10,8},{12,10},{14,12},{0,14},{3,1},{5,3},... | collective-permute-start | bytes 2312 | tf_op jit(solution)/shard_map/ppermute | solution.py:105
  33.4 52.1 %collective-permute-start = (bf16[96,128]{1,0:T(8,128)(2,1)S(1)}, bf16[96,128]{1,0:T(8,128)(2,1)S(1)}, u32[]{:S(2)}, u32[]{:S(2)}) collective-permute-start(bf16[96,128]{1,0:T(8,128)(2,1)S(1)} %slice_bitcast_fusion.2), channel_id=1, source_target_pairs={{1,0},{3,2},{5,4},{7,6},{9,8},{11,10},{13,12},{15,14},{17,16},{19,... | collective-permute-start | bytes 73736 | tf_op jit(solution)/shard_map/ppermute | solution.py:18
  67.8 4.5 %collective-permute-start.2 = (f32[2,96]{1,0:T(2,128)S(1)}, f32[2,96]{1,0:T(2,128)S(1)}, u32[]{:S(2)}, u32[]{:S(2)}) collective-permute-start(f32[2,96]{1,0:T(2,128)S(1)} %collective-permute-done.1), channel_id=1, source_target_pairs={{0,2},{2,4},{4,6},{6,8},{8,10},{10,12},{12,14},{14,0},{1,3},{3,5},... | collective-permute-start | bytes 2312 | tf_op jit(solution)/shard_map/ppermute | solution.py:103
  72.4 4.5 %collective-permute-start.3 = (f32[2,96]{1,0:T(2,128)S(1)}, f32[2,96]{1,0:T(2,128)S(1)}, u32[]{:S(2)}, u32[]{:S(2)}) collective-permute-start(f32[2,96]{1,0:T(2,128)S(1)} %collective-permute-done.2), channel_id=1, source_target_pairs={{0,2},{2,4},{4,6},{6,8},{8,10},{10,12},{12,14},{14,0},{1,3},{3,5},... | collective-permute-start | bytes 2312 | tf_op jit(solution)/shard_map/ppermute | solution.py:103
  72.4 6.2 %collective-permute-start.6 = (f32[2,96]{1,0:T(2,128)S(1)}, f32[2,96]{1,0:T(2,128)S(1)}, u32[]{:S(2)}, u32[]{:S(2)}) collective-permute-start(f32[2,96]{1,0:T(2,128)S(1)} %collective-permute-done.5), channel_id=1, source_target_pairs={{2,0},{4,2},{6,4},{8,6},{10,8},{12,10},{14,12},{0,14},{3,1},{5,3},... | collective-permute-start | bytes 2312 | tf_op jit(solution)/shard_map/ppermute | solution.py:105
  76.8 5.5 %collective-permute-start.4 = (f32[2,96]{1,0:T(2,128)S(1)}, f32[2,96]{1,0:T(2,128)S(1)}, u32[]{:S(2)}, u32[]{:S(2)}) collective-permute-start(f32[2,96]{1,0:T(2,128)S(1)} %collective-permute-done.3), channel_id=1, source_target_pairs={{0,2},{2,4},{4,6},{6,8},{8,10},{10,12},{12,14},{14,0},{1,3},{3,5},... | collective-permute-start | bytes 2312 | tf_op jit(solution)/shard_map/ppermute | solution.py:103
  76.8 0.7 copy-start.4
  78.6 5.0 %collective-permute-start.7 = (f32[2,96]{1,0:T(2,128)S(1)}, f32[2,96]{1,0:T(2,128)S(1)}, u32[]{:S(2)}, u32[]{:S(2)}) collective-permute-start(f32[2,96]{1,0:T(2,128)S(1)} %collective-permute-done.6), channel_id=1, source_target_pairs={{2,0},{4,2},{6,4},{8,6},{10,8},{12,10},{14,12},{0,14},{3,1},{5,3},... | collective-permute-start | bytes 2312 | tf_op jit(solution)/shard_map/ppermute | solution.py:105
  136.0 3.0 %collective-permute-start.8 = (f32[96]{0:T(128)S(1)}, f32[96]{0:T(128)S(1)}, u32[]{:S(2)}, u32[]{:S(2)}) collective-permute-start(f32[96]{0:T(128)S(1)} %slice_bitcast_fusion.3), channel_id=1, source_target_pairs={{1,0},{3,2},{5,4},{7,6},{9,8},{11,10},{13,12},{15,14},{17,16},{19,... | collective-permute-start | bytes 1160 | tf_op jit(solution)/shard_map/ppermute | solution.py:18
Sparse Core Ops, SparseCore 0:
  180.8 88.4 all-reduce.6
